TPU v7x, 32 devices: a whole 2x2x4 slice. The times are simulated.
32 devices in a mesh: lat: 8 (over z, x), gz: 4 (over y, core).
Axes of the slice: x: 2, y: 2, z: 4, core: 2. Of those that a mesh axis runs over, the one named last changes fastest.
Arguments:
- tiles: float32 [8, 1280, 512], P('gz', 'lat'), may hold values from 0.1 to 4.5
- offsets: int32 [8], replicated, may hold values from -32 to 0
- taps_x: float32 [31], replicated, may hold values from 0.01 to 0.1
- taps_y: float32 [31], replicated, may hold values from 0.01 to 0.1
- taps_z: float32 [63], replicated, may hold values from 0.005 to 0.05
Outputs:
- deconvolved: float32 [8, 1024, 512], P('gz', 'lat')
Inputs may be any that keep to these rules, and one draw needn't show every extreme that they name: Tile d's first row belongs at stitched row d * 128 + offsets[d].
All inputs are finite; a program needn't handle non-finite values.
Results may differ from a plain program's by a relative error of at most 0.0001.
Values sent between devices are 32-bit elements; how exact they have to be, the bound alone decides.
A program may use at most 64 MiB of HBM per device.

v0:
```python
import functools

import jax
import jax.numpy as jnp
from jax import lax
from jax.experimental import pallas as pl
from jax.experimental.pallas import tpu as pltpu
from jax.sharding import PartitionSpec as P

SPILL = 32
ITERS = 2
REACH = 16
CHUNKS = 2
LANES = 128
MESH = pl.DeviceIdType.MESH
F32 = jnp.float32
BF16 = jnp.bfloat16


def halves(value):
    high = value.astype(BF16)
    return high, (value - high.astype(F32)).astype(BF16)


def product(left, right):
    (left_high, left_low), (right_high, right_low) = left, right

    def dot(a, b):
        return jnp.dot(a, b, preferred_element_type=F32)

    return dot(left_high, right_high) + (dot(left_high, right_low) + dot(left_low, right_high))


def banded(taps_ref, index):
    def add_tap(k, value):
        return jnp.where(index == k, taps_ref[k], value)

    return lax.fori_loop(0, taps_ref.shape[0], add_tap, jnp.zeros(index.shape, F32))


def shifted_rows(value, amount):
    length = value.shape[0]
    amounts = jnp.zeros(value.shape, jnp.int32) + amount
    bit = 1
    while bit <= SPILL:
        moved = pltpu.roll(value, length - bit, 0)
        value = jnp.where((amounts & bit) != 0, moved, value)
        bit *= 2
    return value[: length - SPILL]


def store_halves(ref, where, value):
    high, low = halves(value)
    ref[(0,) + where] = high
    ref[(1,) + where] = low


def kernel(
    lat_count, gz_count,
    tiles_hbm, offsets_hbm, taps_x_hbm, taps_y_hbm, taps_z_hbm, out_ref,
    tiles_ref, offsets_ref, taps_x_ref, taps_y_ref, taps_z_ref, load_sem,
    shifted, gathered, left_spill, right_spill, observed, estimate, ratio, lateral_y, final,
    x_forward, x_adjoint, yz_forward, yz_adjoint,
    tile_send, tile_recv, left_send, left_recv, right_send, right_recv,
    halo_send, halo_recv, final_send, final_recv, local_sem,
):
    lat, gz = lax.axis_index("lat"), lax.axis_index("gz")
    pairs = ((tiles_hbm, tiles_ref), (offsets_hbm, offsets_ref), (taps_x_hbm, taps_x_ref),
             (taps_y_hbm, taps_y_ref), (taps_z_hbm, taps_z_ref))
    loads = [pltpu.make_async_copy(source, target, load_sem.at[i])
             for i, (source, target) in enumerate(pairs)]
    for load in loads:
        load.start()
    plane_count, tile_rows, width = tiles_ref.shape
    slots, planes, rows, _ = observed.shape
    brick = tile_rows - SPILL
    depth = slots // 2
    spill_blocks = SPILL // rows
    units, _, unit, _ = ratio.shape
    out_rows = units * unit
    total = lat_count * gz_count

    chunk = width // CHUNKS
    chunks = [slice(c * chunk, (c + 1) * chunk) for c in range(CHUNKS)]

    def owner(lat_index, block):
        return jnp.where(lat_index % 2 == 0, block, gz_count - 1 - block)

    block = owner(lat, gz)
    place = lat * gz_count + block

    def device_at(position):
        lat_index = position // gz_count
        return lat_index, owner(lat_index, position % gz_count)

    own_planes = pl.ds(gz * plane_count, plane_count)

    def tile_copy(step, c):
        target = (gz + step) % gz_count
        source_rows = pl.ds(pl.multiple_of(owner(lat, target) * rows, rows), rows)
        return pltpu.make_async_remote_copy(
            shifted.at[:, source_rows, chunks[c]], gathered.at[own_planes, :, chunks[c]],
            tile_send.at[step, c], tile_recv.at[step, c], (lat, target), MESH)

    def right_going(q, c):
        return pltpu.make_async_remote_copy(
            tiles_ref.at[:, brick:tile_rows, chunks[c]],
            left_spill.at[own_planes, 0:SPILL, chunks[c]],
            left_send.at[q, c], left_recv.at[gz, c], (lat + 1, owner(lat + 1, q)), MESH)

    def left_going(q, c):
        return pltpu.make_async_remote_copy(
            tiles_ref.at[:, 0:SPILL, chunks[c]],
            right_spill.at[own_planes, SPILL:2 * SPILL, chunks[c]],
            right_send.at[q, c], right_recv.at[gz, c], (lat - 1, owner(lat - 1, gz_count - 1 - q)), MESH)

    has_right, has_left = lat < lat_count - 1, lat > 0
    others = [e for e in range(-depth, depth + 1) if e != 0]

    def there(e):
        return (place + e >= 0) & (place + e < total)

    barrier = pltpu.get_barrier_semaphore()

    def greet(device):
        pl.semaphore_signal(barrier, inc=1, device_id=device, device_id_type=MESH)

    expected = gz_count - 1 + jnp.where(has_right, spill_blocks, 0) + jnp.where(has_left, spill_blocks, 0)
    for step in range(1, gz_count):
        greet((lat, (gz + step) % gz_count))
    for e in others:
        expected = expected + jnp.where(there(e), 1, 0)

        @pl.when(there(e))
        def _():
            greet(device_at(place + e))

    @pl.when(has_left & (block < spill_blocks))
    def _():
        for source in range(gz_count):
            greet((lat - 1, source))

    @pl.when(has_right & (block >= gz_count - spill_blocks))
    def _():
        for source in range(gz_count):
            greet((lat + 1, source))

    loads[0].wait()
    loads[1].wait()
    own_offset = offsets_ref[lat]
    for plane in range(plane_count):
        shifted[plane] = shifted_rows(tiles_ref[plane], 0 - own_offset)
    pl.semaphore_wait(barrier, expected)

    for c in range(CHUNKS):
        @pl.when(has_right)
        def _():
            for q in range(spill_blocks):
                right_going(q, c).start()

        @pl.when(has_left)
        def _():
            for q in range(spill_blocks):
                left_going(q, c).start()

        for step in range(1, gz_count):
            tile_copy(step, c).start()
    own_rows = pl.ds(pl.multiple_of(block * rows, rows), rows)
    gathered[own_planes] = shifted[:, own_rows, :]

    @pl.when(has_left & (block < spill_blocks))
    def _():
        left_spill[:, SPILL:2 * SPILL, :] = jnp.zeros((planes, SPILL, width), F32)

    @pl.when(has_right & (block >= gz_count - spill_blocks))
    def _():
        right_spill[:, 0:SPILL, :] = jnp.zeros((planes, SPILL, width), F32)

    for e in others:
        @pl.when(jnp.logical_not(there(e)))
        def _():
            observed[depth + e] = jnp.zeros(observed.shape[1:], F32)
            estimate[depth + e] = jnp.zeros(estimate.shape[1:], F32)

    for load in loads[2:]:
        load.wait()
    half_xy = (taps_x_ref.shape[0] - 1) // 2
    half_z = (taps_z_ref.shape[0] - 1) // 2
    blocks = width // LANES
    gap = (lax.broadcasted_iota(jnp.int32, (LANES, LANES), 0)
           - lax.broadcasted_iota(jnp.int32, (LANES, LANES), 1))

    def build_x(matrix, sign):
        matrix[...] = jnp.zeros_like(matrix)
        for delta in (-1, 0, 1):
            value = banded(taps_x_ref, half_xy + sign * (gap + delta * LANES))
            for column in range(blocks):
                row = column + delta
                if 0 <= row < blocks:
                    spot = (slice(row * LANES, (row + 1) * LANES),
                            slice(column * LANES, (column + 1) * LANES))
                    store_halves(matrix, spot, value)

    build_x(x_forward, 1)

    def axial(lane_plane, plane, sign):
        weights = jnp.zeros(lane_plane.shape, F32)
        for other in range(planes):
            tap = taps_z_ref[half_z + sign * (other - plane)]
            weights = jnp.where(lane_plane == other, tap, weights)
        return weights

    lanes = lax.broadcasted_iota(jnp.int32, (out_rows, planes * rows), 1)
    out_ids = lax.broadcasted_iota(jnp.int32, (out_rows, planes * rows), 0)
    lane_row = lanes % rows
    lane_plane = (lax.broadcasted_iota(jnp.int32, (8, planes * rows), 1)) // rows

    def reached(slot):
        start = (slot - depth) * rows + REACH - half_xy
        return max(0, start // unit), min(units, (start + rows + 2 * half_xy - 1) // unit + 1)

    def build_axial(z, carry):
        weights = axial(lane_plane, z, 1)[0:1]
        for slot in range(slots):
            block_value = lateral_y[slot] * weights
            for u in range(*reached(slot)):
                spot = (slot, pl.ds(pl.multiple_of((u * planes + z) * unit, unit), unit), slice(None))
                store_halves(yz_forward, spot, block_value[u * unit:(u + 1) * unit])
        return carry

    for slot in range(slots):
        index = lane_row + (slot - depth) * rows - (out_ids - REACH) + half_xy
        lateral_y[slot] = banded(taps_y_ref, index)
    lax.fori_loop(0, planes, build_axial, 0)

    wide = planes * out_rows

    def build_adjoint():
        build_x(x_adjoint, -1)
        lane = lax.broadcasted_iota(jnp.int32, (rows, wide), 1)
        row_ids = lax.broadcasted_iota(jnp.int32, (rows, wide), 0)
        back_lateral = banded(taps_y_ref, half_xy - (lane // (unit * planes) * unit + lane % unit - REACH - row_ids))
        wide_plane = lax.broadcasted_iota(jnp.int32, (8, wide), 1) // unit % planes
        for z in range(planes):
            weights = axial(wide_plane, z, -1)[0:1]
            store_halves(yz_adjoint, (slice(z * rows, (z + 1) * rows), slice(None)), back_lateral * weights)

    left_offset = offsets_ref[jnp.maximum(lat - 1, 0)]
    right_offset = offsets_ref[jnp.minimum(lat + 1, lat_count - 1)]
    brick_rows = block * rows + lax.broadcasted_iota(jnp.int32, (rows, chunk), 0)
    from_left = has_left & (brick_rows < SPILL + left_offset)
    from_right = has_right & (brick_rows >= brick + right_offset)
    counts = 1.0 + jnp.where(from_left, 1.0, 0.0) + jnp.where(from_right, 1.0, 0.0)

    def halo_copy(buffer, which, e, c):
        return pltpu.make_async_remote_copy(
            buffer.at[depth, :, :, chunks[c]], buffer.at[depth - e, :, :, chunks[c]],
            halo_send.at[which, depth - e, c], halo_recv.at[which, depth - e, c],
            device_at(place + e), MESH)

    def send_halos(buffer, which, c):
        for e in others:
            @pl.when(there(e))
            def _():
                halo_copy(buffer, which, e, c).start()

    for c in range(CHUNKS):
        for step in range(1, gz_count):
            tile_copy(step, c).wait_recv()

        @pl.when(has_left & (block < spill_blocks))
        def _():
            for source in range(gz_count):
                sent = slice(source * plane_count, (source + 1) * plane_count)
                part = left_spill.at[sent, 0:SPILL, chunks[c]]
                pltpu.make_async_copy(part, part, left_recv.at[source, c]).wait()
            reach = pl.ds(pl.multiple_of(block * rows, 8), rows + SPILL)
            for z in range(planes):
                spill = left_spill[z, reach, chunks[c]]
                gathered[z, :, chunks[c]] += shifted_rows(spill, 0 - left_offset)

        @pl.when(has_right & (block >= gz_count - spill_blocks))
        def _():
            for source in range(gz_count):
                sent = slice(source * plane_count, (source + 1) * plane_count)
                part = right_spill.at[sent, SPILL:2 * SPILL, chunks[c]]
                pltpu.make_async_copy(part, part, right_recv.at[source, c]).wait()
            first = (block - (gz_count - spill_blocks)) * rows
            reach = pl.ds(pl.multiple_of(first, 8), rows + SPILL)
            for z in range(planes):
                spill = right_spill[z, reach, chunks[c]]
                gathered[z, :, chunks[c]] += shifted_rows(spill, 0 - right_offset)

        for z in range(planes):
            observed[depth, z, :, chunks[c]] = gathered[z, :, chunks[c]] / counts
        send_halos(observed, 0, c)

    build_adjoint()

    def final_copy(step, c):
        target = (gz + step) % gz_count
        return pltpu.make_async_remote_copy(
            final.at[pl.ds(target * plane_count, plane_count), :, chunks[c]],
            out_ref.at[:, own_rows, chunks[c]],
            final_send.at[step, c], final_recv.at[step, c], (lat, target), MESH)

    for which, buffer in zip(range(ITERS), [observed] + [estimate] * (ITERS - 1)):
        def part(slot, c):
            first, last = reached(slot)
            spot = slice(first * planes * unit, last * planes * unit)
            data = halves(buffer[slot, :, :, chunks[c]].reshape(planes * rows, chunk))
            value = product((yz_forward[0, slot, spot], yz_forward[1, slot, spot]), data)
            return {u: value[(u - first) * planes * unit:(u + 1 - first) * planes * unit]
                    for u in range(first, last)}

        sums = [part(depth, c) for c in range(CHUNKS)]
        blurred = None
        for c in range(CHUNKS):
            lateral = sums[c]
            for e in others:
                @pl.when(there(e))
                def _():
                    halo_copy(buffer, which, 0 - e, c).wait_recv()
                for u, value in part(depth + e, c).items():
                    lateral[u] = lateral[u] + value if u in lateral else value
            lateral = jnp.concatenate([lateral[u] for u in range(units)], 0)
            term = product(halves(lateral), (x_forward[0, chunks[c], :], x_forward[1, chunks[c], :]))
            blurred = term if blurred is None else blurred + term
        blurred = blurred.reshape(units, planes, unit, width)
        for u in range(units):
            row = u * unit - REACH + depth * rows
            slot, first = row // rows, row % rows
            quotient = observed[slot, :, first:first + unit, :] / blurred[u]
            ratio[u] = jnp.where(there(slot - depth), quotient, 0.0)
        data = halves(ratio[...].reshape(wide, width))
        back = halves(product((yz_adjoint[0], yz_adjoint[1]), data))
        for c in range(CHUNKS):
            gain = product(back, (x_adjoint[0, :, chunks[c]], x_adjoint[1, :, chunks[c]]))
            value = buffer[depth, :, :, chunks[c]] * gain.reshape(planes, rows, chunk)
            if which < ITERS - 1:
                estimate[depth, :, :, chunks[c]] = value
                send_halos(estimate, which + 1, c)
            else:
                final[:, :, chunks[c]] = value
                for step in range(1, gz_count):
                    final_copy(step, c).start()

    mine = pltpu.make_async_copy(final.at[own_planes], out_ref.at[:, own_rows, :], local_sem)
    mine.start()

    for c in range(CHUNKS):
        for step in range(1, gz_count):
            tile_copy(step, c).wait_send()

        @pl.when(has_right)
        def _():
            for q in range(spill_blocks):
                right_going(q, c).wait_send()

        @pl.when(has_left)
        def _():
            for q in range(spill_blocks):
                left_going(q, c).wait_send()

        for which, buffer in zip(range(ITERS), [observed] + [estimate] * (ITERS - 1)):
            for e in others:
                @pl.when(there(e))
                def _():
                    halo_copy(buffer, which, e, c).wait_send()

        for step in range(1, gz_count):
            final_copy(step, c).wait()
    mine.wait()


def local(lat_count, gz_count, tiles, offsets, taps_x, taps_y, taps_z):
    plane_count, tile_rows, width = tiles.shape
    brick = tile_rows - SPILL
    rows = brick // gz_count
    planes = plane_count * gz_count
    depth = 2 * REACH // rows
    slots = 2 * depth + 1
    out_rows = rows + 2 * REACH
    unit = 16 if rows % 16 == 0 else 8
    spill_blocks = SPILL // rows
    dma = pltpu.SemaphoreType.DMA
    hbm = pl.BlockSpec(memory_space=pltpu.HBM)
    return pl.pallas_call(
        functools.partial(kernel, lat_count, gz_count),
        out_shape=jax.ShapeDtypeStruct((plane_count, brick, width), F32),
        in_specs=[hbm] * 5,
        out_specs=pl.BlockSpec(memory_space=pl.ANY),
        scratch_shapes=[
            pltpu.VMEM(tiles.shape, F32), pltpu.SMEM(offsets.shape, jnp.int32),
            pltpu.SMEM(taps_x.shape, F32), pltpu.SMEM(taps_y.shape, F32),
            pltpu.SMEM(taps_z.shape, F32), dma((5,)),
            pltpu.VMEM((plane_count, brick, width), F32),
            pltpu.VMEM((planes, rows, width), F32),
            pltpu.VMEM((planes, 2 * SPILL, width), F32),
            pltpu.VMEM((planes, 2 * SPILL, width), F32),
            pltpu.VMEM((slots, planes, rows, width), F32),
            pltpu.VMEM((slots, planes, rows, width), F32),
            pltpu.VMEM((out_rows // unit, planes, unit, width), F32),
            pltpu.VMEM((slots, out_rows, planes * rows), F32),
            pltpu.VMEM((planes, rows, width), F32),
            pltpu.VMEM((2, width, width), BF16),
            pltpu.VMEM((2, width, width), BF16),
            pltpu.VMEM((2, slots, planes * out_rows, planes * rows), BF16),
            pltpu.VMEM((2, planes * rows, planes * out_rows), BF16),
            dma((gz_count, CHUNKS)), dma((gz_count, CHUNKS)),
            dma((spill_blocks, CHUNKS)), dma((gz_count, CHUNKS)),
            dma((spill_blocks, CHUNKS)), dma((gz_count, CHUNKS)),
            dma((ITERS, slots, CHUNKS)), dma((ITERS, slots, CHUNKS)),
            dma((gz_count, CHUNKS)), dma((gz_count, CHUNKS)), dma,
        ],
        compiler_params=pltpu.CompilerParams(
            has_side_effects=True, collective_id=0, vmem_limit_bytes=60 * 1024 * 1024),
    )(tiles, offsets, taps_x, taps_y, taps_z)


def solution(mesh):
    in_specs = (P("gz", "lat", None), P(), P(), P(), P())
    out_specs = P("gz", "lat", None)
    body = functools.partial(local, mesh.shape["lat"], mesh.shape["gz"])
    return jax.shard_map(body, mesh=mesh, in_specs=in_specs, out_specs=out_specs, check_vma=False)
```

profile of v0, /device:TPU:0, one launch (start us, length us, event | category | flops | bytes accessed | tf_op | source)
XLA Modules:
  0.0 40.9 jit_solution(4981575109894295700)
XLA Ops:
  0.0 39.0 %shard_map.55 = f32[2,128,512]{2,1,0:T(8,128)} custom-call(f32[2,160,512]{2,1,0:T(8,128)} %tiles_hbm.1, s32[8]{0:T(128)} %offsets_hbm.1, f32[31]{0:T(128)} %taps_x_hbm.1, f32[31]{0:T(128)} %taps_y_hbm.1, f32[63]{0:T(128)} %taps_z_hbm.1), custom_call_target="tpu_custom_call" | custom-call | tf_op jit(solution)/shard_map/pallas_call | solution.py:388
  39.0 1.9 %copy.7 = f32[2,128,512]{2,1,0:T(8,128)} copy(f32[2,128,512]{2,1,0:T(8,128)} %shard_map.55) | data formatting | bytes 1048576
where the time goes:
time: 41.1 us; the launch traced here: 40.9 us
  Pallas kernels  39 us (95%)
  local copies, waits for them, and re-layouts  1.87 us (5%)
    pallas_call x1, Pallas kernels, local(): pl.pallas_call(functools.partial(kernel, lat_count, gz_count), out_shape=...  39 us
    unnamed x1, local copies, waits for them, and re-layouts  1.87 us

commit v1 on v0

--- a/solution.py
+++ b/solution.py
@@ -12,6 +12,8 @@
 REACH = 16
 CHUNKS = 2
 LANES = 128
+UNIT = 2 * REACH
+VMEM_LIMIT = 60 * 1024 * 1024
 MESH = pl.DeviceIdType.MESH
 F32 = jnp.float32
 BF16 = jnp.bfloat16
@@ -373,7 +375,7 @@
     mine.wait()
 
 
-def local(lat_count, gz_count, tiles, offsets, taps_x, taps_y, taps_z):
+def by_rows(lat_count, gz_count, tiles, offsets, taps_x, taps_y, taps_z):
     plane_count, tile_rows, width = tiles.shape
     brick = tile_rows - SPILL
     rows = brick // gz_count
@@ -418,6 +420,451 @@
     )(tiles, offsets, taps_x, taps_y, taps_z)
 
 
+def column_of(lane, outside):
+    left, right = LANES + UNIT, LANES + 2 * UNIT
+    return jnp.where(lane < LANES, lane,
+                     jnp.where(lane < left, lane - left, jnp.where(lane < right, lane - UNIT, outside)))
+
+
+def strip_kernel(
+    lat_count, gz_count,
+    tiles_hbm, offsets_hbm, taps_x_hbm, taps_y_hbm, taps_z_hbm, out_ref,
+    tiles_ref, offsets_ref, taps_x_ref, taps_y_ref, taps_z_ref, load_sem,
+    raw, spill_out, spill_in, observed, estimate, parts, quotient, edges, halo, final,
+    x_forward, x_adjoint, yz_forward, yz_adjoint,
+    tile_send, tile_recv, spill_send, spill_recv, row_send, row_recv,
+    side_send, side_recv, final_send, final_recv,
+):
+    lat, gz = lax.axis_index("lat"), lax.axis_index("gz")
+    pairs = ((tiles_hbm, tiles_ref), (offsets_hbm, offsets_ref), (taps_x_hbm, taps_x_ref),
+             (taps_y_hbm, taps_y_ref), (taps_z_hbm, taps_z_ref))
+    loads = [pltpu.make_async_copy(source, target, load_sem.at[i])
+             for i, (source, target) in enumerate(pairs)]
+    for load in loads:
+        load.start()
+    plane_count, tile_rows, width = tiles_ref.shape
+    planes, brick, _ = final.shape
+    blocks = brick // UNIT
+    strips = gz_count
+    groups = edges.shape[2]
+    pack = planes // groups
+    lane_x, core = lat % 2, gz % 2
+    brick_id = lat - lane_x + core
+    strip = jnp.where(lane_x == 0, gz // 2, strips - 1 - gz // 2)
+    at_home = core == lane_x
+
+    def device(brick_index, s):
+        column = jnp.where(s < strips // 2, 0, 1)
+        row = jnp.where(s < strips // 2, s, strips - 1 - s)
+        return brick_index - brick_index % 2 + column, 2 * row + brick_index % 2
+
+    has_up, has_down = brick_id > 0, brick_id < lat_count - 1
+    has_left, has_right = strip > 0, strip < strips - 1
+    vertical = {-1: has_up, 1: has_down}
+    sideways = {-1: has_left, 1: has_right}
+
+    def when(condition, action):
+        pl.when(condition)(action)
+
+    barrier = pltpu.get_barrier_semaphore()
+
+    def greet(target):
+        pl.semaphore_signal(barrier, inc=1, device_id=target, device_id_type=MESH)
+
+    for step in range(1, 2 * gz_count):
+        position = (lane_x * gz_count + gz + step) % (2 * gz_count)
+        greet((lat - lane_x + position // gz_count, position % gz_count))
+    expected = 2 * gz_count - 1
+    outward = jnp.where(core == 0, -1, 1)
+    has_outward = jnp.where(core == 0, brick_id, lat_count - 1 - brick_id) > 0
+    for shift in (-1, 0, 1):
+        condition = has_outward if shift == 0 else has_outward & sideways[shift]
+        expected = expected + jnp.where(condition, 1, 0)
+        when(condition, lambda shift=shift: greet(device(brick_id + outward, strip + shift)))
+
+    side_rows = [slice(q * UNIT, (q + 1) * UNIT) for q in range(blocks + 2)]
+
+    def clear_up():
+        spill_in[0] = jnp.zeros(spill_in.shape[1:], F32)
+        observed[:, side_rows[0], 0:LANES] = jnp.zeros((planes, UNIT, LANES), F32)
+        estimate[:, :, side_rows[0], :] = jnp.zeros((ITERS - 1, planes, UNIT, LANES), F32)
+        halo[:, :, :, side_rows[0], :] = jnp.zeros((ITERS, 2, groups, UNIT, LANES), F32)
+
+    def clear_down():
+        spill_in[1] = jnp.zeros(spill_in.shape[1:], F32)
+        observed[:, side_rows[-1], 0:LANES] = jnp.zeros((planes, UNIT, LANES), F32)
+        estimate[:, :, side_rows[-1], :] = jnp.zeros((ITERS - 1, planes, UNIT, LANES), F32)
+        halo[:, :, :, side_rows[-1], :] = jnp.zeros((ITERS, 2, groups, UNIT, LANES), F32)
+
+    def clear_side(side):
+        halo[:, side] = jnp.zeros((ITERS, *halo.shape[2:]), F32)
+
+    when(jnp.logical_not(has_up), clear_up)
+    when(jnp.logical_not(has_down), clear_down)
+    when(jnp.logical_not(has_left), lambda: clear_side(0))
+    when(jnp.logical_not(has_right), lambda: clear_side(1))
+    raw[:, 0:SPILL, :] = jnp.zeros((planes, SPILL, LANES), F32)
+    raw[:, SPILL + tile_rows:, :] = jnp.zeros((planes, SPILL, LANES), F32)
+
+    pieces = (slice(0, SPILL), slice(brick, tile_rows), slice(SPILL, brick))
+    own_planes = pl.ds(gz * plane_count, plane_count)
+
+    def lanes_of(s):
+        return pl.ds(pl.multiple_of(s * LANES, LANES), LANES)
+
+    def landed(piece):
+        return slice(SPILL + piece.start, SPILL + piece.stop)
+
+    def tile_copy(step, i):
+        s = (strip + step) % strips
+        return pltpu.make_async_remote_copy(
+            tiles_ref.at[:, pieces[i], lanes_of(s)], raw.at[own_planes, landed(pieces[i]), :],
+            tile_send.at[step, i], tile_recv.at[gz, i], device(lat, s), MESH)
+
+    def tile_stay(i):
+        return pltpu.make_async_copy(
+            tiles_ref.at[:, pieces[i], lanes_of(strip)], raw.at[own_planes, landed(pieces[i]), :],
+            tile_recv.at[gz, i])
+
+    def arrived(part, semaphore):
+        pltpu.make_async_copy(part, part, semaphore).wait()
+
+    def tile_wait(i):
+        for source in range(gz_count):
+            sent = slice(source * plane_count, (source + 1) * plane_count)
+            arrived(raw.at[sent, landed(pieces[i]), :], tile_recv.at[source, i])
+
+    def send_tiles(steps, numbers):
+        for i in numbers:
+            for step in steps:
+                if step > 0:
+                    tile_copy(step, i).start()
+                else:
+                    when(at_home, lambda i=i: tile_stay(i).start())
+                    when(jnp.logical_not(at_home), lambda i=i: tile_copy(0, i).start())
+
+    loads[0].wait()
+    pl.semaphore_wait(barrier, expected)
+    send_tiles((*range(1, strips), 0), range(len(pieces)))
+
+    for load in loads[1:]:
+        load.wait()
+    half_x = (taps_x_ref.shape[0] - 1) // 2
+    half_y = (taps_y_ref.shape[0] - 1) // 2
+    half_z = (taps_z_ref.shape[0] - 1) // 2
+    far = 1 << 20
+
+    def build_x(matrix, sign):
+        _, depth, breadth = matrix.shape
+        tall = LANES // 2
+        for start in range(0, depth, tall):
+            inner = start + lax.broadcasted_iota(jnp.int32, (tall, breadth), 0)
+            outer = lax.broadcasted_iota(jnp.int32, (tall, breadth), 1)
+            gap = column_of(inner, far) - column_of(outer, 0 - far)
+            high, low = halves(banded(taps_x_ref, half_x + sign * gap))
+            matrix[0, start:start + tall, :] = high
+            matrix[1, start:start + tall, :] = low
+
+    tall, deep = planes * UNIT, planes * 2 * UNIT
+
+    def build_yz(matrix, sign):
+        lane = lax.broadcasted_iota(jnp.int32, (UNIT, deep), 1)
+        row = lax.broadcasted_iota(jnp.int32, (UNIT, deep), 0)
+        lateral = banded(taps_y_ref, half_y + sign * (lane % (2 * UNIT) - row) - REACH * sign)
+        lane_plane = lax.broadcasted_iota(jnp.int32, (8, deep), 1) // (2 * UNIT)
+        for z in range(planes):
+            weights = jnp.zeros(lane_plane.shape, F32)
+            for other in range(planes):
+                weights = jnp.where(lane_plane == other, taps_z_ref[half_z + sign * (other - z)], weights)
+            high, low = halves(lateral * weights[0:1])
+            matrix[z * UNIT:(z + 1) * UNIT, :] = high
+            matrix[tall + z * UNIT:tall + (z + 1) * UNIT, :] = low
+
+    build_x(x_forward, 1)
+    build_yz(yz_forward, 1)
+
+    own_offset = offsets_ref[brick_id]
+    up_offset = offsets_ref[jnp.maximum(brick_id - 1, 0)]
+    down_offset = offsets_ref[jnp.minimum(brick_id + 1, lat_count - 1)]
+
+    def spill_copy(i):
+        return pltpu.make_async_remote_copy(
+            spill_out.at[i], spill_in.at[1 - i], spill_send.at[i], spill_recv.at[1 - i],
+            device(brick_id + 2 * i - 1, strip), MESH)
+
+    def placed(first):
+        return [shifted_rows(raw[z, first:first + UNIT + SPILL, :], 0 - own_offset) for z in range(planes)]
+
+    for i, condition in enumerate((has_up, has_down)):
+        tile_wait(i)
+        for z, value in enumerate(placed(i * (tile_rows))):
+            spill_out[i, z] = value
+        when(condition, lambda i=i: spill_copy(i).start())
+
+    lane_ids = lax.broadcasted_iota(jnp.int32, (UNIT, LANES), 1)
+
+    def current(which):
+        return observed if which == 0 else estimate.at[which - 1]
+
+    def row_copy(which, way):
+        source = side_rows[1] if way < 0 else side_rows[blocks]
+        target = side_rows[blocks + 1] if way < 0 else side_rows[0]
+        i = (way + 1) // 2
+        buffer = current(which)
+        return pltpu.make_async_remote_copy(
+            buffer.at[:, source, 0:LANES], buffer.at[:, target, 0:LANES],
+            row_send.at[which, i], row_recv.at[which, i], device(brick_id + way, strip), MESH)
+
+    def side_copy(which, shift, way, block):
+        side = (1 - shift) // 2
+        q = block + 1 if way == 0 else (blocks + 1 if way < 0 else 0)
+        return pltpu.make_async_remote_copy(
+            edges.at[which, side, :, block * UNIT:(block + 1) * UNIT, :],
+            halo.at[which, side, :, side_rows[q], :],
+            side_send.at[which, side, q], side_recv.at[which, side, q],
+            device(brick_id + way, strip + shift), MESH)
+
+    def all_copies(which, block):
+        ways = ([-1] if block == 0 else []) + ([1] if block == blocks - 1 else [])
+        copies = []
+        for way in ways:
+            for shift in (1, -1):
+                copies.append((sideways[shift] & vertical[way], side_copy(which, shift, way, block)))
+            copies.append((vertical[way], row_copy(which, way)))
+        for shift in (1, -1):
+            copies.append((sideways[shift], side_copy(which, shift, 0, block)))
+        return copies
+
+    def keep(which, block, values):
+        rows = side_rows[block + 1]
+        spot = slice(block * UNIT, (block + 1) * UNIT)
+        buffer = current(which)
+        for group in range(groups):
+            right = left = None
+            for j in range(pack):
+                z = group * pack + j
+                value = values[z]
+                buffer[z, rows, 0:LANES] = value
+                store_halves(parts.at[which], (z, rows, slice(0, LANES)), value)
+                moved = pltpu.roll(value, (UNIT * (j + 1)) % LANES, 1) if j + 1 < pack else value
+                right = moved if right is None else jnp.where(lane_ids // UNIT == j, moved, right)
+                moved = pltpu.roll(value, UNIT * j, 1) if j > 0 else value
+                left = moved if left is None else jnp.where(lane_ids // UNIT == j, moved, left)
+            edges[which, 0, group, spot, :] = right
+            edges[which, 1, group, spot, :] = left
+        for condition, copy in all_copies(which, block):
+            when(condition, lambda copy=copy: copy.start())
+
+    def absorb(which, q):
+        rows = side_rows[q]
+        way = -1 if q == 0 else (1 if q == blocks + 1 else 0)
+        buffer = current(which)
+        if way != 0:
+            when(vertical[way], lambda: arrived(buffer.at[:, rows, 0:LANES], row_recv.at[which, (1 - way) // 2]))
+            for z in range(planes):
+                store_halves(parts.at[which], (z, rows, slice(0, LANES)), buffer[z, rows, 0:LANES])
+        for side, condition in enumerate((has_left, has_right)):
+            condition = condition if way == 0 else condition & vertical[way]
+            when(condition, lambda side=side: arrived(
+                halo.at[which, side, :, rows, :], side_recv.at[which, side, q]))
+        for group in range(groups):
+            from_left, from_right = halo[which, 0, group, rows, :], halo[which, 1, group, rows, :]
+            for j in range(pack):
+                z = group * pack + j
+                left = pltpu.roll(from_left, LANES - UNIT * j, 1) if j > 0 else from_left
+                right = pltpu.roll(from_right, (LANES + UNIT - UNIT * j) % LANES, 1) if j != 1 else from_right
+                value = jnp.where(lane_ids < UNIT, left, jnp.where(lane_ids < 2 * UNIT, right, 0.0))
+                if which == 0:
+                    observed[z, rows, LANES:2 * LANES] = value
+                store_halves(parts.at[which], (z, rows, slice(LANES, 2 * LANES)), value)
+
+    def dot(a, b):
+        return jnp.dot(a, b, preferred_element_type=F32)
+
+    def apply_yz(matrix, data_ref, first):
+        high, low = [data_ref[i, :, first:first + 2 * UNIT, :].reshape(deep, 2 * LANES) for i in (0, 1)]
+        both = dot(matrix[...], high)
+        return both[:tall] + (both[tall:] + dot(matrix[:tall, :], low))
+
+    def apply_x(value, matrix):
+        high, low = halves(value)
+        both = dot(jnp.concatenate([high, low], 0), matrix[0])
+        return both[:tall] + (both[tall:] + dot(high, matrix[1]))
+
+    wide_lane = lax.broadcasted_iota(jnp.int32, (UNIT, 2 * LANES), 1)
+    wide_row = lax.broadcasted_iota(jnp.int32, (UNIT, 2 * LANES), 0)
+    inside_columns = ((wide_lane < LANES)
+                      | (has_left & (wide_lane >= LANES) & (wide_lane < LANES + UNIT))
+                      | (has_right & (wide_lane >= LANES + UNIT) & (wide_lane < LANES + 2 * UNIT)))
+
+    def forward(which, k):
+        blurred = apply_x(apply_yz(yz_forward, parts.at[which], k * UNIT), x_forward)
+        inside = inside_columns
+        if k == 0:
+            inside = inside & (has_up | (wide_row >= REACH))
+        if k == blocks:
+            inside = inside & (has_down | (wide_row < UNIT - REACH))
+        for z in range(planes):
+            start = k * UNIT + UNIT - REACH
+            value = observed[z, start:start + UNIT, :] / blurred[z * UNIT:(z + 1) * UNIT]
+            store_halves(quotient, (z, slice(k * UNIT, (k + 1) * UNIT), slice(None)),
+                         jnp.where(inside, value, 0.0))
+
+    def final_copy(step, block):
+        target = (gz + step) % gz_count
+        rows = slice(block * UNIT, (block + 1) * UNIT)
+        return pltpu.make_async_remote_copy(
+            final.at[pl.ds(target * plane_count, plane_count), rows, :],
+            out_ref.at[:, rows, lanes_of(strip)],
+            final_send.at[step, block], final_recv.at[strip, block], (brick_id, target), MESH)
+
+    def final_stay(block):
+        rows = slice(block * UNIT, (block + 1) * UNIT)
+        return pltpu.make_async_copy(
+            final.at[own_planes, rows, :], out_ref.at[:, rows, lanes_of(strip)], final_recv.at[strip, block])
+
+    def adjoint(which, block):
+        gain = apply_x(apply_yz(yz_adjoint, quotient, block * UNIT), x_adjoint)
+        buffer = current(which)
+        values = [buffer[z, side_rows[block + 1], 0:LANES] * gain[z * UNIT:(z + 1) * UNIT] for z in range(planes)]
+        if which < ITERS - 1:
+            keep(which + 1, block, values)
+            return
+        for z in range(planes):
+            final[z, block * UNIT:(block + 1) * UNIT, :] = values[z]
+        for step in range(1, gz_count):
+            final_copy(step, block).start()
+        when(at_home, lambda: final_stay(block).start())
+        when(jnp.logical_not(at_home), lambda: final_copy(0, block).start())
+
+    build_x(x_adjoint, -1)
+    build_yz(yz_adjoint, -1)
+    tile_wait(len(pieces) - 1)
+    inner = list(range(1, blocks - 1))
+    row_ids = lax.broadcasted_iota(jnp.int32, (UNIT, LANES), 0)
+
+    def drain_tiles():
+        for i in range(len(pieces)):
+            for step in range(1, strips):
+                tile_copy(step, i).wait_send()
+            when(jnp.logical_not(at_home), lambda i=i: tile_copy(0, i).wait_send())
+        for i, condition in enumerate((has_up, has_down)):
+            when(condition, lambda i=i: spill_copy(i).wait_send())
+
+    def drain_blocks(which):
+        for block in range(blocks):
+            for condition, copy in all_copies(which, block):
+                when(condition, lambda copy=copy: copy.wait_send())
+
+    def start_block(block):
+        values = placed(SPILL + block * UNIT)
+        for i, (edge, condition) in enumerate(((0, has_up), (blocks - 1, has_down))):
+            if block == edge:
+                when(condition, lambda i=i: arrived(spill_in.at[i], spill_recv.at[i]))
+                limit = SPILL + up_offset - block * UNIT if i == 0 else brick + down_offset - block * UNIT
+                shared = has_up & (row_ids < limit) if i == 0 else has_down & (row_ids >= limit)
+                counts = jnp.where(shared, 2.0, 1.0)
+                values = [(value + spill_in[i, z]) / counts for z, value in enumerate(values)]
+        keep(0, block, values)
+
+    start_block(1)
+    start_block(2)
+    start_block(0)
+    start_block(3)
+    drain_tiles()
+    absorb(0, 2)
+    absorb(0, 3)
+    forward(0, 2)
+    absorb(0, 1)
+    forward(0, 1)
+    adjoint(0, 1)
+    absorb(0, 4)
+    forward(0, 3)
+    adjoint(0, 2)
+    absorb(0, 0)
+    forward(0, 0)
+    adjoint(0, 0)
+    absorb(0, 5)
+    forward(0, 4)
+    adjoint(0, 3)
+    drain_blocks(0)
+    absorb(1, 2)
+    absorb(1, 3)
+    forward(1, 2)
+    absorb(1, 1)
+    forward(1, 1)
+    adjoint(1, 1)
+    absorb(1, 4)
+    forward(1, 3)
+    adjoint(1, 2)
+    absorb(1, 0)
+    forward(1, 0)
+    adjoint(1, 0)
+    absorb(1, 5)
+    forward(1, 4)
+    adjoint(1, 3)
+    drain_blocks(ITERS - 1)
+    for s in range(strips):
+        for block in range(blocks):
+            part = out_ref.at[:, block * UNIT:(block + 1) * UNIT, s * LANES:(s + 1) * LANES]
+            arrived(part, final_recv.at[s, block])
+    for block in range(blocks):
+        for step in range(1, gz_count):
+            final_copy(step, block).wait_send()
+        when(jnp.logical_not(at_home), lambda block=block: final_copy(0, block).wait_send())
+
+
+def by_strips(lat_count, gz_count, tiles, offsets, taps_x, taps_y, taps_z):
+    plane_count, tile_rows, width = tiles.shape
+    brick = tile_rows - SPILL
+    planes = plane_count * gz_count
+    groups = planes // (LANES // UNIT)
+    blocks = brick // UNIT
+    tall, deep = planes * UNIT, planes * 2 * UNIT
+    dma = pltpu.SemaphoreType.DMA
+    hbm = pl.BlockSpec(memory_space=pltpu.HBM)
+    return pl.pallas_call(
+        functools.partial(strip_kernel, lat_count, gz_count),
+        out_shape=jax.ShapeDtypeStruct((plane_count, brick, width), F32),
+        in_specs=[hbm] * 5,
+        out_specs=pl.BlockSpec(memory_space=pl.ANY),
+        scratch_shapes=[
+            pltpu.VMEM(tiles.shape, F32), pltpu.SMEM(offsets.shape, jnp.int32),
+            pltpu.SMEM(taps_x.shape, F32), pltpu.SMEM(taps_y.shape, F32),
+            pltpu.SMEM(taps_z.shape, F32), dma((5,)),
+            pltpu.VMEM((planes, tile_rows + 2 * SPILL, LANES), F32),
+            pltpu.VMEM((2, planes, SPILL, LANES), F32),
+            pltpu.VMEM((2, planes, SPILL, LANES), F32),
+            pltpu.VMEM((planes, brick + 2 * UNIT, 2 * LANES), F32),
+            pltpu.VMEM((ITERS - 1, planes, brick + 2 * UNIT, LANES), F32),
+            pltpu.VMEM((ITERS, 2, planes, brick + 2 * UNIT, 2 * LANES), BF16),
+            pltpu.VMEM((2, planes, brick + UNIT, 2 * LANES), BF16),
+            pltpu.VMEM((ITERS, 2, groups, brick, LANES), F32),
+            pltpu.VMEM((ITERS, 2, groups, brick + 2 * UNIT, LANES), F32),
+            pltpu.VMEM((planes, brick, LANES), F32),
+            pltpu.VMEM((2, 2 * LANES, 2 * LANES), BF16),
+            pltpu.VMEM((2, 2 * LANES, LANES), BF16),
+            pltpu.VMEM((2 * tall, deep), BF16),
+            pltpu.VMEM((2 * tall, deep), BF16),
+            dma((gz_count, 3)), dma((gz_count, 3)), dma((2,)), dma((2,)),
+            dma((ITERS, 2)), dma((ITERS, 2)),
+            dma((ITERS, 2, blocks + 2)), dma((ITERS, 2, blocks + 2)),
+            dma((gz_count, blocks)), dma((gz_count, blocks)),
+        ],
+        compiler_params=pltpu.CompilerParams(
+            has_side_effects=True, collective_id=0, vmem_limit_bytes=VMEM_LIMIT),
+    )(tiles, offsets, taps_x, taps_y, taps_z)
+
+
+def local(lat_count, gz_count, tiles, offsets, taps_x, taps_y, taps_z):
+    plane_count, tile_rows, width = tiles.shape
+    brick, planes = tile_rows - SPILL, plane_count * gz_count
+    fits = (width == gz_count * LANES and gz_count % 2 == 0 and lat_count % 2 == 0
+            and planes % (LANES // UNIT) == 0 and brick % UNIT == 0 and brick >= 4 * UNIT)
+    arrange = by_strips if fits else by_rows
+    return arrange(lat_count, gz_count, tiles, offsets, taps_x, taps_y, taps_z)
+
+
 def solution(mesh):
     in_specs = (P("gz", "lat", None), P(), P(), P(), P())
     out_specs = P("gz", "lat", None)

time: 41.1 us -> 40.4 us (0.983)
  Pallas kernels: 39 us -> 38.3 us
    pallas_call x1, Pallas kernels: 39 us -> 38.3 us  [by_strips(): pl.pallas_call(functools.partial(strip_kernel, lat_count, gz_count), out_...]
where the time goes in v1:
time: 40.4 us; the launch traced here: 40.2 us
  Pallas kernels  38.3 us (95%)
  local copies, waits for them, and re-layouts  1.87 us (5%)
    pallas_call x1, Pallas kernels, by_strips(): pl.pallas_call(functools.partial(strip_kernel, lat_count, gz_count), out_...  38.3 us
    unnamed x1, local copies, waits for them, and re-layouts  1.87 us

profile of v1, /device:TPU:0, one launch (start us, length us, event | category | flops | bytes accessed | tf_op | source)
XLA Modules:
  0.0 40.2 jit_solution(15832069071342838180)
XLA Ops:
  0.0 38.3 %shard_map.55 = f32[2,128,512]{2,1,0:T(8,128)} custom-call(f32[2,160,512]{2,1,0:T(8,128)} %tiles_hbm.1, s32[8]{0:T(128)} %offsets_hbm.1, f32[31]{0:T(128)} %taps_x_hbm.1, f32[31]{0:T(128)} %taps_y_hbm.1, f32[63]{0:T(128)} %taps_z_hbm.1), custom_call_target="tpu_custom_call" | custom-call | tf_op jit(solution)/shard_map/pallas_call | solution.py:826
  38.4 1.9 %copy.7 = f32[2,128,512]{2,1,0:T(8,128)} copy(f32[2,128,512]{2,1,0:T(8,128)} %shard_map.55) | data formatting | bytes 1048576

commit v2 on v1

--- a/solution.py
+++ b/solution.py
@@ -430,7 +430,7 @@
     lat_count, gz_count,
     tiles_hbm, offsets_hbm, taps_x_hbm, taps_y_hbm, taps_z_hbm, out_ref,
     tiles_ref, offsets_ref, taps_x_ref, taps_y_ref, taps_z_ref, load_sem,
-    raw, spill_out, spill_in, observed, estimate, parts, quotient, edges, halo, final,
+    raw, spill_out, spill_in, observed, estimate, parts, middle, quotient, edges, halo, final,
     x_forward, x_adjoint, yz_forward, yz_adjoint,
     tile_send, tile_recv, spill_send, spill_recv, row_send, row_recv,
     side_send, side_recv, final_send, final_recv,
@@ -652,6 +652,8 @@
                 left = moved if left is None else jnp.where(lane_ids // UNIT == j, moved, left)
             edges[which, 0, group, spot, :] = right
             edges[which, 1, group, spot, :] = left
+
+    def send_block(which, block):
         for condition, copy in all_copies(which, block):
             when(condition, lambda copy=copy: copy.start())
 
@@ -681,15 +683,15 @@
     def dot(a, b):
         return jnp.dot(a, b, preferred_element_type=F32)
 
-    def apply_yz(matrix, data_ref, first):
+    def apply_yz(matrix, data_ref, first, slot):
         high, low = [data_ref[i, :, first:first + 2 * UNIT, :].reshape(deep, 2 * LANES) for i in (0, 1)]
         both = dot(matrix[...], high)
-        return both[:tall] + (both[tall:] + dot(matrix[:tall, :], low))
-
-    def apply_x(value, matrix):
-        high, low = halves(value)
-        both = dot(jnp.concatenate([high, low], 0), matrix[0])
-        return both[:tall] + (both[tall:] + dot(high, matrix[1]))
+        value = both[:tall] + (both[tall:] + dot(matrix[:tall, :], low))
+        middle[slot, :tall, :], middle[slot, tall:, :] = halves(value)
+
+    def apply_x(matrix, slot):
+        both = dot(middle[slot], matrix[0])
+        return both[:tall] + (both[tall:] + dot(middle[slot, :tall, :], matrix[1]))
 
     wide_lane = lax.broadcasted_iota(jnp.int32, (UNIT, 2 * LANES), 1)
     wide_row = lax.broadcasted_iota(jnp.int32, (UNIT, 2 * LANES), 0)
@@ -697,8 +699,11 @@
                       | (has_left & (wide_lane >= LANES) & (wide_lane < LANES + UNIT))
                       | (has_right & (wide_lane >= LANES + UNIT) & (wide_lane < LANES + 2 * UNIT)))
 
-    def forward(which, k):
-        blurred = apply_x(apply_yz(yz_forward, parts.at[which], k * UNIT), x_forward)
+    def forward_yz(which, k, slot):
+        apply_yz(yz_forward, parts.at[which], k * UNIT, slot)
+
+    def forward_x(which, k, slot):
+        blurred = apply_x(x_forward, slot)
         inside = inside_columns
         if k == 0:
             inside = inside & (has_up | (wide_row >= REACH))
@@ -723,8 +728,11 @@
         return pltpu.make_async_copy(
             final.at[own_planes, rows, :], out_ref.at[:, rows, lanes_of(strip)], final_recv.at[strip, block])
 
-    def adjoint(which, block):
-        gain = apply_x(apply_yz(yz_adjoint, quotient, block * UNIT), x_adjoint)
+    def adjoint_yz(which, block, slot):
+        apply_yz(yz_adjoint, quotient, block * UNIT, slot)
+
+    def adjoint_x(which, block, slot):
+        gain = apply_x(x_adjoint, slot)
         buffer = current(which)
         values = [buffer[z, side_rows[block + 1], 0:LANES] * gain[z * UNIT:(z + 1) * UNIT] for z in range(planes)]
         if which < ITERS - 1:
@@ -732,6 +740,11 @@
             return
         for z in range(planes):
             final[z, block * UNIT:(block + 1) * UNIT, :] = values[z]
+
+    def send_result(which, block):
+        if which < ITERS - 1:
+            send_block(which + 1, block)
+            return
         for step in range(1, gz_count):
             final_copy(step, block).start()
         when(at_home, lambda: final_stay(block).start())
@@ -766,6 +779,7 @@
                 counts = jnp.where(shared, 2.0, 1.0)
                 values = [(value + spill_in[i, z]) / counts for z, value in enumerate(values)]
         keep(0, block, values)
+        send_block(0, block)
 
     start_block(1)
     start_block(2)
@@ -774,35 +788,61 @@
     drain_tiles()
     absorb(0, 2)
     absorb(0, 3)
-    forward(0, 2)
     absorb(0, 1)
-    forward(0, 1)
-    adjoint(0, 1)
     absorb(0, 4)
-    forward(0, 3)
-    adjoint(0, 2)
+    forward_yz(0, 2, 0)
+    forward_yz(0, 1, 1)
+    forward_x(0, 2, 0)
+    forward_yz(0, 3, 0)
+    forward_x(0, 1, 1)
+    adjoint_yz(0, 1, 2)
+    forward_x(0, 3, 0)
+    adjoint_yz(0, 2, 3)
+    adjoint_x(0, 1, 2)
+    adjoint_x(0, 2, 3)
+    send_result(0, 1)
+    send_result(0, 2)
     absorb(0, 0)
-    forward(0, 0)
-    adjoint(0, 0)
     absorb(0, 5)
-    forward(0, 4)
-    adjoint(0, 3)
+    forward_yz(0, 0, 1)
+    forward_yz(0, 4, 0)
+    forward_x(0, 0, 1)
+    forward_x(0, 4, 0)
+    adjoint_yz(0, 0, 2)
+    adjoint_yz(0, 3, 3)
+    adjoint_x(0, 0, 2)
+    send_result(0, 0)
+    adjoint_x(0, 3, 3)
+    send_result(0, 3)
     drain_blocks(0)
     absorb(1, 2)
     absorb(1, 3)
-    forward(1, 2)
     absorb(1, 1)
-    forward(1, 1)
-    adjoint(1, 1)
+    forward_yz(1, 2, 0)
+    forward_yz(1, 1, 1)
+    forward_x(1, 2, 0)
+    forward_x(1, 1, 1)
+    adjoint_yz(1, 1, 2)
     absorb(1, 4)
-    forward(1, 3)
-    adjoint(1, 2)
+    forward_yz(1, 3, 0)
+    adjoint_x(1, 1, 2)
+    send_result(1, 1)
+    forward_x(1, 3, 0)
+    adjoint_yz(1, 2, 3)
     absorb(1, 0)
-    forward(1, 0)
-    adjoint(1, 0)
+    forward_yz(1, 0, 1)
+    adjoint_x(1, 2, 3)
+    send_result(1, 2)
+    forward_x(1, 0, 1)
+    adjoint_yz(1, 0, 2)
     absorb(1, 5)
-    forward(1, 4)
-    adjoint(1, 3)
+    forward_yz(1, 4, 0)
+    adjoint_x(1, 0, 2)
+    send_result(1, 0)
+    forward_x(1, 4, 0)
+    adjoint_yz(1, 3, 3)
+    adjoint_x(1, 3, 3)
+    send_result(1, 3)
     drain_blocks(ITERS - 1)
     for s in range(strips):
         for block in range(blocks):
@@ -838,6 +878,7 @@
             pltpu.VMEM((planes, brick + 2 * UNIT, 2 * LANES), F32),
             pltpu.VMEM((ITERS - 1, planes, brick + 2 * UNIT, LANES), F32),
             pltpu.VMEM((ITERS, 2, planes, brick + 2 * UNIT, 2 * LANES), BF16),
+            pltpu.VMEM((4, 2 * tall, 2 * LANES), BF16),
             pltpu.VMEM((2, planes, brick + UNIT, 2 * LANES), BF16),
             pltpu.VMEM((ITERS, 2, groups, brick, LANES), F32),
             pltpu.VMEM((ITERS, 2, groups, brick + 2 * UNIT, LANES), F32),

time: 40.4 us -> 39 us (0.965)
  Pallas kernels: 38.3 us -> 36.9 us
    pallas_call x1, Pallas kernels: 38.3 us -> 36.9 us  [by_strips(): pl.pallas_call(functools.partial(strip_kernel, lat_count, gz_count), out_...]
where the time goes in v2:
time: 39 us; the launch traced here: 38.8 us
  Pallas kernels  36.9 us (95%)
  local copies, waits for them, and re-layouts  1.87 us (5%)
    pallas_call x1, Pallas kernels, by_strips(): pl.pallas_call(functools.partial(strip_kernel, lat_count, gz_count), out_...  36.9 us
    unnamed x1, local copies, waits for them, and re-layouts  1.87 us

profile of v2, /device:TPU:0, one launch (start us, length us, event | category | flops | bytes accessed | tf_op | source)
XLA Modules:
  0.0 38.8 jit_solution(6214926042681051046)
XLA Ops:
  0.0 36.9 %shard_map.55 = f32[2,128,512]{2,1,0:T(8,128)} custom-call(f32[2,160,512]{2,1,0:T(8,128)} %tiles_hbm.1, s32[8]{0:T(128)} %offsets_hbm.1, f32[31]{0:T(128)} %taps_x_hbm.1, f32[31]{0:T(128)} %taps_y_hbm.1, f32[63]{0:T(128)} %taps_z_hbm.1), custom_call_target="tpu_custom_call" | custom-call | tf_op jit(solution)/shard_map/pallas_call | solution.py:866
  36.9 1.9 %copy.7 = f32[2,128,512]{2,1,0:T(8,128)} copy(f32[2,128,512]{2,1,0:T(8,128)} %shard_map.55) | data formatting | bytes 1048576

commit v3 on v2

--- a/solution.py
+++ b/solution.py
@@ -626,13 +626,11 @@
 
     def all_copies(which, block):
         ways = ([-1] if block == 0 else []) + ([1] if block == blocks - 1 else [])
-        copies = []
+        copies = [(sideways[shift], side_copy(which, shift, 0, block)) for shift in (1, -1)]
         for way in ways:
             for shift in (1, -1):
                 copies.append((sideways[shift] & vertical[way], side_copy(which, shift, way, block)))
             copies.append((vertical[way], row_copy(which, way)))
-        for shift in (1, -1):
-            copies.append((sideways[shift], side_copy(which, shift, 0, block)))
         return copies
 
     def keep(which, block, values):

time: 39 us -> 38.6 us (0.990)
  no operation moved by 1% of the time
where the time goes in v3:
time: 38.6 us; the launch traced here: 38.4 us
  Pallas kernels  36.6 us (95%)
  local copies, waits for them, and re-layouts  1.87 us (5%)
    pallas_call x1, Pallas kernels, by_strips(): pl.pallas_call(functools.partial(strip_kernel, lat_count, gz_count), out_...  36.6 us
    unnamed x1, local copies, waits for them, and re-layouts  1.87 us

profile of v3, /device:TPU:0, one launch (start us, length us, event | category | flops | bytes accessed | tf_op | source)
XLA Modules:
  0.0 38.4 jit_solution(3153326861342401998)
XLA Ops:
  0.0 36.6 %shard_map.55 = f32[2,128,512]{2,1,0:T(8,128)} custom-call(f32[2,160,512]{2,1,0:T(8,128)} %tiles_hbm.1, s32[8]{0:T(128)} %offsets_hbm.1, f32[31]{0:T(128)} %taps_x_hbm.1, f32[31]{0:T(128)} %taps_y_hbm.1, f32[63]{0:T(128)} %taps_z_hbm.1), custom_call_target="tpu_custom_call" | custom-call | tf_op jit(solution)/shard_map/pallas_call | solution.py:864
  36.6 1.9 %copy.7 = f32[2,128,512]{2,1,0:T(8,128)} copy(f32[2,128,512]{2,1,0:T(8,128)} %shard_map.55) | data formatting | bytes 1048576
